TPU v7x, 128 devices: a whole 4x4x4 slice. The times are simulated.
128 devices in a mesh: wa: 16 (over x, z), ha: 8 (over y, core).
Axes of the slice: x: 4, y: 4, z: 4, core: 2. Of those that a mesh axis runs over, the one named last changes fastest.
Arguments:
- tokens: bfloat16 [512, 16384], P('ha', 'wa'), may hold values from -100 to 100, as said below
- norm_gain: float32 [16384], P('wa'), may hold values from 0.5 to 1.5
- gate_weight: bfloat16 [16384, 26624], P('wa', 'ha'), may hold values from -0.046875 to 0.046875
- up_weight: bfloat16 [16384, 26624], P('wa', 'ha'), may hold values from -0.046875 to 0.046875
- down_weight: bfloat16 [26624, 16384], P('ha', 'wa'), may hold values from -0.0390625 to 0.0390625
Outputs:
- mixed: bfloat16 [512, 16384], P('ha', 'wa')
Inputs may be any that keep to these rules, and one draw needn't show every extreme that they name: `tokens`: real-valued activations.
All inputs are finite; a program needn't handle non-finite values.
Results may differ from a plain program's by a relative error of at most 0.0064.
Values may be sent and summed in bfloat16 or wider, within the bound.
A program may use at most 128 MiB of HBM per device.

v0:
```python
import jax
import jax.numpy as jnp
from jax import lax
from jax.sharding import PartitionSpec as P


def apply_norm(own_values, squares, norm_gain):
    model_width = own_values.shape[1] * lax.axis_size("wa")
    mean_square = squares[:, None] / model_width
    return (own_values * lax.rsqrt(mean_square + 1e-05) * norm_gain[None, :]).astype(jnp.bfloat16)


def activate(summed, hidden_width):
    gate = summed[:, :hidden_width]
    up = summed[:, hidden_width:]
    return (jax.nn.silu(gate) * up).astype(jnp.bfloat16)


def body(tokens, norm_gain, gate_weight, up_weight, down_weight):
    gathered = lax.all_gather(tokens, "ha", axis=0, tiled=True)
    own_values = gathered.astype(jnp.float32)
    squares = lax.psum(jnp.sum(own_values * own_values, axis=1), "wa")
    normed = apply_norm(own_values, squares, norm_gain)
    hidden_width = gate_weight.shape[1]
    gate_part = jnp.dot(normed, gate_weight, preferred_element_type=jnp.float32)
    up_part = jnp.dot(normed, up_weight, preferred_element_type=jnp.float32)
    summed = lax.psum_scatter(
        jnp.concatenate([gate_part, up_part], axis=1), "wa", scatter_dimension=0, tiled=True
    )
    hidden = activate(summed, hidden_width)
    partial_out = jnp.dot(
        lax.all_gather(hidden, "wa", axis=0, tiled=True),
        down_weight,
        preferred_element_type=jnp.float32,
    )
    mixed_out = lax.psum_scatter(partial_out, "ha", scatter_dimension=0, tiled=True)
    return mixed_out.astype(jnp.bfloat16)


def solution(mesh):
    placed = (P("ha", "wa"), P("wa"), P("wa", "ha"), P("wa", "ha"), P("ha", "wa"))
    return jax.shard_map(body, mesh=mesh, in_specs=placed, out_specs=P("ha", "wa"), check_vma=False)
```

profile of v0, /device:TPU:0, one launch (start us, length us, event | category | flops | bytes accessed | tf_op | source)
XLA Modules:
  0.0 285.8 jit_solution(6064925622431984980)
XLA Ops:
  6.5 0.0 all-gather.3.cloned.1.call-start
  6.5 0.7 all-gather.3.cloned.1.call-update
  7.3 0.0 reduce-scatter.3.cloned.1.call-start
  7.3 27.6 %all-gather.3.cloned.1.call-done = bf16[512,1024]{1,0:T(8,128)(2,1)} async-done(((bf16[64,1024]{1,0:T(8,128)(2,1)}), bf16[512,1024]{1,0:T(8,128)(2,1)}) %all-gather.3.cloned.1.call-update) | async-done | bytes 1048592 | tf_op jit(solution)/shard_map/all_gather | solution.py:20
  34.9 1.7 fusion
  36.6 40.5 %psum.7 = f32[512]{0:T(512)S(1)} all-reduce(f32[512]{0:T(512)S(1)} %fusion), channel_id=1, replica_groups=mesh['wa'=16,'ha'=8] {'wa'}, use_global_device_ids=true, to_apply=%region_1.0 | all-reduce | flops 512 | bytes 4096 | tf_op jit(solution)/shard_map/psum | solution.py:22
  77.1 0.0 copy-start.1
  77.1 6.7 %fusion.4 = f32[512,3328]{1,0:T(8,128)S(1)} fusion(bf16[1024,3328]{1,0:T(8,128)(2,1)} %param.8, bf16[512,1024]{1,0:T(8,128)(2,1)} %all-gather.3.cloned.1.call-done, f32[1024]{0:T(1024)} %param.6, f32[512]{0:T(512)S(1)} %add_rsqrt_fusion), kind=kOutput, calls=%fused_computation.8 | convolution fusion | flops 3491758080 | bytes 14686208 | tf_op jit(solution)/shard_map/dot_general | solution.py:26
  83.9 0.0 slice-done
  83.9 0.0 copy-done
  83.9 0.0 slice-done.1
  83.9 3.8 %fusion.6 = f32[512,3328]{1,0:T(8,128)S(1)} fusion(bf16[1024,3328]{1,0:T(8,128)(2,1)S(1)} %bitcast.5, bf16[512,1024]{1,0:T(8,128)(2,1)S(1)} %copy-done, f32[1024]{0:T(1024)S(1)} %copy-done.1, f32[512]{0:T(512)S(1)} %add_rsqrt_fusion), kind=kOutput, calls=%fused_computation.9 | convolution fusion | flops 3491758080 | bytes 14686208 | tf_op jit(solution)/shard_map/dot_general | solution.py:25
  87.8 5.4 %pad_maximum_fusion = f32[512,6656]{1,0:T(8,128)} fusion(f32[512,3328]{1,0:T(8,128)S(1)} %fusion.4, f32[512,3328]{1,0:T(8,128)S(1)} %fusion.6), kind=kLoop, calls=%fused_computation | loop fusion | flops 3407872 | bytes 27262976 | tf_op jit(solution)/shard_map/concatenate | solution.py:28
  93.2 0.0 reduce-scatter.3.cloned.1.call-update
  93.2 0.0 all-gather.5.cloned.1.call-start
  93.3 92.7 %reduce-scatter.3.cloned.1.call-done = f32[32,6656]{1,0:T(8,128)} async-done(((f32[512,6656]{1,0:T(8,128)}), f32[32,6656]{1,0:T(8,128)}) %reduce-scatter.3.cloned.1.call-update) | async-done | bytes 851984 | tf_op jit(solution)/shard_map/reduce_scatter | solution.py:27
  185.9 1.9 fusion.3
  187.9 0.0 all-gather.5.cloned.1.call-update
  187.9 0.0 reduce-scatter.5.cloned.1.call-start
  187.9 48.1 %all-gather.5.cloned.1.call-done = bf16[512,3328]{1,0:T(8,128)(2,1)} async-done(((bf16[32,3328]{1,0:T(8,128)(2,1)}), bf16[512,3328]{1,0:T(8,128)(2,1)}) %all-gather.5.cloned.1.call-update) | async-done | bytes 3407888 | tf_op jit(solution)/shard_map/all_gather | solution.py:32
  236.1 9.0 %fusion.8 = f32[512,1024]{1,0:T(8,128)} fusion(bf16[512,3328]{1,0:T(8,128)(2,1)} %all-gather.5.cloned.1.call-done, bf16[3328,1024]{1,0:T(8,128)(2,1)} %param.9), kind=kOutput, calls=%fused_computation.11 | convolution fusion | flops 3489660928 | bytes 12320768 | tf_op jit(solution)/shard_map/dot_general | solution.py:31
  245.1 0.0 reduce-scatter.5.cloned.1.call-update
  245.1 32.6 %reduce-scatter.5.cloned.1.call-done = f32[64,1024]{1,0:T(8,128)} async-done(((f32[512,1024]{1,0:T(8,128)}), f32[64,1024]{1,0:T(8,128)}) %reduce-scatter.5.cloned.1.call-update) | async-done | bytes 262160 | tf_op jit(solution)/shard_map/reduce_scatter | solution.py:36
  277.7 1.6 convert_element_type.15
  (6 shorter events, 0.0 us)
Async XLA Ops:
  6.5 28.4 %all-gather.3.cloned.1.call-start = ((), (), s32[]{:S(2)}) async-start(), calls=%async_computation.2 | async-start | bytes 1179648 | tf_op jit(solution)/shard_map/all_gather | solution.py:20
  7.3 178.7 %reduce-scatter.3.cloned.1.call-start = ((), (), s32[]{:S(2)}) async-start(), calls=%async_computation.3 | async-start | bytes 14483456 | tf_op jit(solution)/shard_map/reduce_scatter | solution.py:27
  34.9 48.9 %slice-start = ((s8[6815744]{0:T(1024)(128)(4,1)}), s8[2621440]{0:T(1024)(128)(4,1)S(1)}, s32[]{:S(2)}) async-start(s8[6815744]{0:T(1024)(128)(4,1)} %bitcast.4), calls=%async_computation.6 | async-start | bytes 5242880
  77.1 6.8 %copy-start = (bf16[512,1024]{1,0:T(8,128)(2,1)S(1)}, bf16[512,1024]{1,0:T(8,128)(2,1)}, u32[]{:S(2)}) copy-start(bf16[512,1024]{1,0:T(8,128)(2,1)} %all-gather.3.cloned.1.call-done) | copy-start | bytes 3145732
  77.1 6.8 %slice-start.1 = ((s8[6815744]{0:T(1024)(128)(4,1)}), s8[4194304]{0:T(1024)(128)(4,1)S(1)}, s32[]{:S(2)}) async-start(s8[6815744]{0:T(1024)(128)(4,1)} %bitcast.4), calls=%async_computation.7 | async-start | bytes 8388608
  77.1 6.8 %copy-start.1 = (f32[1024]{0:T(1024)S(1)}, f32[1024]{0:T(1024)}, u32[]{:S(2)}) copy-start(f32[1024]{0:T(1024)} %param.6) | copy-start | bytes 12292
  93.2 142.8 %all-gather.5.cloned.1.call-start = ((), (), s32[]{:S(2)}) async-start(), calls=%async_computation.4 | async-start | bytes 3620864 | tf_op jit(solution)/shard_map/all_gather | solution.py:32
  187.9 89.8 %reduce-scatter.5.cloned.1.call-start = ((), (), s32[]{:S(2)}) async-start(), calls=%async_computation.5 | async-start | bytes 2359296 | tf_op jit(solution)/shard_map/reduce_scatter | solution.py:36
Sparse Core Ops, SparseCore 0:
  9.1 25.8 all-gather.2
  93.3 92.5 reduce-scatter.2
  188.4 47.6 all-gather.4
  245.2 32.3 reduce-scatter.4
where the time goes:
time: 286 us
  waiting for transfers between devices  202 us (71%)
  blocking collectives  40.5 us (14%)
  matrix products  19.5 us (7%)
  between operations  13.2 us (5%)
  other arithmetic  10.7 us (4%)
    reduce_scatter x1, waiting for transfers between devices, body(): lax.psum_scatter(jnp.concatenate([gate_part, up_part], axis=1), 'wa', sca...  92.7 us
    all_gather x1, waiting for transfers between devices, body(): lax.all_gather(hidden, 'wa', axis=0, tiled=True)  48.1 us
    psum x1, blocking collectives, body(): squares = lax.psum(jnp.sum(own_values * own_values, axis=1), 'wa')  40.5 us
    reduce_scatter x1, waiting for transfers between devices, body(): lax.psum_scatter(partial_out, 'ha', scatter_dimension=0, tiled=True)  32.6 us
    all_gather x1, waiting for transfers between devices, body(): gathered = lax.all_gather(tokens, 'ha', axis=0, tiled=True)  27.6 us
    dot_general x1, matrix products, body(): jnp.dot(lax.all_gather(hidden, 'wa', axis=0, tiled=True), down_weight, pr...  9 us
    dot_general x1, matrix products, body(): up_part = jnp.dot(normed, up_weight, preferred_element_type=jnp.float32)  6.72 us
  transfers between devices with their start and end apart: 4, of which 4 were waited for; matrix products, arithmetic and copies ran while one was open for 0% of the time, Pallas kernels for 0%

commit v1 on v0

--- a/solution.py
+++ b/solution.py
@@ -2,6 +2,11 @@
 import jax.numpy as jnp
 from jax import lax
 from jax.sharding import PartitionSpec as P
+
+
+def gather_and_add(array, axis):
+    parts = lax.all_gather(array, axis)
+    return jnp.sum(parts, axis=0)
 
 
 def apply_norm(own_values, squares, norm_gain):
@@ -19,7 +24,7 @@
 def body(tokens, norm_gain, gate_weight, up_weight, down_weight):
     gathered = lax.all_gather(tokens, "ha", axis=0, tiled=True)
     own_values = gathered.astype(jnp.float32)
-    squares = lax.psum(jnp.sum(own_values * own_values, axis=1), "wa")
+    squares = gather_and_add(jnp.sum(own_values * own_values, axis=1), "wa")
     normed = apply_norm(own_values, squares, norm_gain)
     hidden_width = gate_weight.shape[1]
     gate_part = jnp.dot(normed, gate_weight, preferred_element_type=jnp.float32)

time: 286 us -> 273 us (0.955)
  blocking collectives: 40.5 us -> 23.5 us
  waiting for transfers between devices: 202 us -> 205 us
    psum x1 -> x0, blocking collectives: 40.5 us -> none  [body(): squares = lax.psum(jnp.sum(own_values * own_values, axis=1), 'wa')]
    all_gather x0 -> x1, blocking collectives: none -> 23.5 us  [gather_and_add(): parts = lax.all_gather(array, axis)]
    reduce_scatter x1, waiting for transfers between devices: 92.7 us -> 95.7 us  [body(): lax.psum_scatter(jnp.concatenate([gate_part, up_part], axis=1), 'wa', sca...]
where the time goes in v1:
time: 273 us
  waiting for transfers between devices  205 us (75%)
  blocking collectives  23.5 us (9%)
  matrix products  20.2 us (7%)
  between operations  13.2 us (5%)
  other arithmetic  10.7 us (4%)
    reduce_scatter x1, waiting for transfers between devices, body(): lax.psum_scatter(jnp.concatenate([gate_part, up_part], axis=1), 'wa', sca...  95.7 us
    all_gather x1, waiting for transfers between devices, body(): lax.all_gather(hidden, 'wa', axis=0, tiled=True)  48.1 us
    reduce_scatter x1, waiting for transfers between devices, body(): lax.psum_scatter(partial_out, 'ha', scatter_dimension=0, tiled=True)  32.6 us
    all_gather x1, waiting for transfers between devices, body(): gathered = lax.all_gather(tokens, 'ha', axis=0, tiled=True)  27.6 us
    all_gather x1, blocking collectives, gather_and_add(): parts = lax.all_gather(array, axis)  23.5 us
    dot_general x1, matrix products, body(): jnp.dot(lax.all_gather(hidden, 'wa', axis=0, tiled=True), down_weight, pr...  9 us
    dot_general x1, matrix products, body(): up_part = jnp.dot(normed, up_weight, preferred_element_type=jnp.float32)  7.42 us
  transfers between devices with their start and end apart: 4, of which 4 were waited for; matrix products, arithmetic and copies ran while one was open for 0% of the time, Pallas kernels for 0%

profile of v1, /device:TPU:0, one launch (start us, length us, event | category | flops | bytes accessed | tf_op | source)
XLA Modules:
  0.0 272.5 jit_solution(6042366554275755285)
XLA Ops:
  6.5 0.0 all-gather.5.cloned.1.call-start
  6.5 0.7 all-gather.5.cloned.1.call-update
  7.3 0.0 reduce-scatter.3.cloned.1.call-start
  7.3 27.6 %all-gather.5.cloned.1.call-done = bf16[512,1024]{1,0:T(8,128)(2,1)} async-done(((bf16[64,1024]{1,0:T(8,128)(2,1)}), bf16[512,1024]{1,0:T(8,128)(2,1)}) %all-gather.5.cloned.1.call-update) | async-done | bytes 1048592 | tf_op jit(solution)/shard_map/all_gather | solution.py:25
  34.9 1.7 fusion
  36.6 23.5 %all-gather.1 = f32[16,1,512]{2,1,0:T(1,128)S(1)} all-gather(f32[1,1,512]{2,1,0:T(1,128)S(1)} %bitcast.5), channel_id=2, replica_groups=mesh['wa'=16,'ha'=8] {'wa'}, dimensions={0}, use_global_device_ids=true | all-gather | bytes 34816 | tf_op jit(solution)/shard_map/all_gather | solution.py:8
  60.1 0.0 slice-start.1
  60.2 0.0 copy-start.1
  60.2 7.4 %fusion.4 = f32[512,3328]{1,0:T(8,128)S(1)} fusion(bf16[1024,3328]{1,0:T(8,128)(2,1)} %param.8, bf16[512,1024]{1,0:T(8,128)(2,1)} %all-gather.5.cloned.1.call-done, f32[1024]{0:T(1024)} %param.6, f32[512]{0:T(512)S(1)} %add_rsqrt_fusion), kind=kOutput, calls=%fused_computation.8 | convolution fusion | flops 3491758080 | bytes 14686208 | tf_op jit(solution)/shard_map/dot_general | solution.py:31
  67.6 0.0 slice-done
  67.6 0.0 copy-done
  67.6 3.8 %fusion.6 = f32[512,3328]{1,0:T(8,128)S(1)} fusion(bf16[1024,3328]{1,0:T(8,128)(2,1)S(1)} %bitcast.7, bf16[512,1024]{1,0:T(8,128)(2,1)S(1)} %copy-done, f32[1024]{0:T(1024)S(1)} %copy-done.1, f32[512]{0:T(512)S(1)} %add_rsqrt_fusion), kind=kOutput, calls=%fused_computation.9 | convolution fusion | flops 3491758080 | bytes 14686208 | tf_op jit(solution)/shard_map/dot_general | solution.py:30
  71.4 5.4 %pad_maximum_fusion = f32[512,6656]{1,0:T(8,128)} fusion(f32[512,3328]{1,0:T(8,128)S(1)} %fusion.4, f32[512,3328]{1,0:T(8,128)S(1)} %fusion.6), kind=kLoop, calls=%fused_computation | loop fusion | flops 3407872 | bytes 27262976 | tf_op jit(solution)/shard_map/concatenate | solution.py:33
  76.9 0.0 reduce-scatter.3.cloned.1.call-update
  76.9 0.0 all-gather.7.cloned.1.call-start
  77.0 95.7 %reduce-scatter.3.cloned.1.call-done = f32[32,6656]{1,0:T(8,128)} async-done(((f32[512,6656]{1,0:T(8,128)}), f32[32,6656]{1,0:T(8,128)}) %reduce-scatter.3.cloned.1.call-update) | async-done | bytes 851984 | tf_op jit(solution)/shard_map/reduce_scatter | solution.py:32
  172.6 1.9 fusion.3
  174.6 0.0 all-gather.7.cloned.1.call-update
  174.6 0.0 reduce-scatter.5.cloned.1.call-start
  174.7 48.1 %all-gather.7.cloned.1.call-done = bf16[512,3328]{1,0:T(8,128)(2,1)} async-done(((bf16[32,3328]{1,0:T(8,128)(2,1)}), bf16[512,3328]{1,0:T(8,128)(2,1)}) %all-gather.7.cloned.1.call-update) | async-done | bytes 3407888 | tf_op jit(solution)/shard_map/all_gather | solution.py:37
  222.8 9.0 %fusion.8 = f32[512,1024]{1,0:T(8,128)} fusion(bf16[512,3328]{1,0:T(8,128)(2,1)} %all-gather.7.cloned.1.call-done, bf16[3328,1024]{1,0:T(8,128)(2,1)} %param.9), kind=kOutput, calls=%fused_computation.11 | convolution fusion | flops 3489660928 | bytes 12320768 | tf_op jit(solution)/shard_map/dot_general | solution.py:36
  231.8 0.0 reduce-scatter.5.cloned.1.call-update
  231.8 32.6 %reduce-scatter.5.cloned.1.call-done = f32[64,1024]{1,0:T(8,128)} async-done(((f32[512,1024]{1,0:T(8,128)}), f32[64,1024]{1,0:T(8,128)}) %reduce-scatter.5.cloned.1.call-update) | async-done | bytes 262160 | tf_op jit(solution)/shard_map/reduce_scatter | solution.py:41
  264.4 1.6 convert_element_type.15
  (7 shorter events, 0.1 us)
Async XLA Ops:
  6.5 28.4 %all-gather.5.cloned.1.call-start = ((), (), s32[]{:S(2)}) async-start(), calls=%async_computation.2 | async-start | bytes 1179648 | tf_op jit(solution)/shard_map/all_gather | solution.py:25
  7.3 165.4 %reduce-scatter.3.cloned.1.call-start = ((), (), s32[]{:S(2)}) async-start(), calls=%async_computation.3 | async-start | bytes 14483456 | tf_op jit(solution)/shard_map/reduce_scatter | solution.py:32
  34.9 32.7 %slice-start = ((s8[6815744]{0:T(1024)(128)(4,1)}), s8[2621440]{0:T(1024)(128)(4,1)S(1)}, s32[]{:S(2)}) async-start(s8[6815744]{0:T(1024)(128)(4,1)} %bitcast.6), calls=%async_computation.6 | async-start | bytes 5242880
  60.1 7.5 %copy-start = (bf16[512,1024]{1,0:T(8,128)(2,1)S(1)}, bf16[512,1024]{1,0:T(8,128)(2,1)}, u32[]{:S(2)}) copy-start(bf16[512,1024]{1,0:T(8,128)(2,1)} %all-gather.5.cloned.1.call-done) | copy-start | bytes 3145732
  60.1 7.5 %slice-start.1 = ((s8[6815744]{0:T(1024)(128)(4,1)}), s8[4194304]{0:T(1024)(128)(4,1)S(1)}, s32[]{:S(2)}) async-start(s8[6815744]{0:T(1024)(128)(4,1)} %bitcast.6), calls=%async_computation.7 | async-start | bytes 8388608
  60.2 7.5 %copy-start.1 = (f32[1024]{0:T(1024)S(1)}, f32[1024]{0:T(1024)}, u32[]{:S(2)}) copy-start(f32[1024]{0:T(1024)} %param.6) | copy-start | bytes 12292
  76.9 145.9 %all-gather.7.cloned.1.call-start = ((), (), s32[]{:S(2)}) async-start(), calls=%async_computation.4 | async-start | bytes 3620864 | tf_op jit(solution)/shard_map/all_gather | solution.py:37
  174.6 89.7 %reduce-scatter.5.cloned.1.call-start = ((), (), s32[]{:S(2)}) async-start(), calls=%async_computation.5 | async-start | bytes 2359296 | tf_op jit(solution)/shard_map/reduce_scatter | solution.py:41
Sparse Core Ops, SparseCore 0:
  9.1 25.8 all-gather.4
  77.0 95.5 reduce-scatter.2
  175.1 47.6 all-gather.6
  231.9 32.3 reduce-scatter.4
